TPU v7x, 128 devices: a whole 4x4x4 slice. The times are simulated.
128 devices in a mesh: rows: 32 (over x, z, core), rel: 4 (over y).
Axes of the slice: x: 4, y: 4, z: 4, core: 2. Of those that a mesh axis runs over, the one named last changes fastest.
Arguments:
- features: bfloat16 [16384, 256], P('rows'), may hold values from -6 to 6
- bases: bfloat16 [8, 256, 256], replicated, may hold values from -0.125 to 0.125
- root: bfloat16 [256, 256], replicated, may hold values from -0.375 to 0.375
- coeffs: float32 [800, 8], P('rel'), may hold values from -4 to 4
- tiles: bfloat16 [32, 4, 64, 128, 128], P('rows', 'rel'), as said below
- tile_dst: int32 [32, 4, 64], P('rows', 'rel'), may hold values from 0 to 3
- tile_src: int32 [32, 4, 64], P('rows', 'rel'), may hold values from 0 to 63
- tile_rel: int32 [32, 4, 64], P('rows', 'rel'), may hold values from 0 to 199
- tile_live: int32 [32, 4], P('rows', 'rel'), may hold values from 16 to 64, as said below
- send_list: int32 [32, 4, 32, 2], P('rows', 'rel'), may hold values from 0 to 3
- cotangent: bfloat16 [16384, 256], P('rows'), may hold values from -6 to 6
Outputs:
- output: bfloat16 [16384, 256], P('rows')
- feature_grad: float32 [16384, 256], P('rows')
- basis_grad: float32 [8, 256, 256], replicated
- root_grad: float32 [256, 256], replicated
Inputs may be any that keep to these rules, and one draw needn't show every extreme that they name: `tile_live`: at least one device uses all 64 tile slots. `tiles`: entries are zero or positive, at most 12 / sqrt(2048).
All inputs are finite; a program needn't handle non-finite values.
Results may differ from a plain program's by a relative error of at most 0.0029.
Values may be sent and summed in bfloat16 or wider, within the bound.
A program may use at most 128 MiB of HBM per device.

v0:
```python
import math
import jax
import jax.numpy as jnp
from jax import lax
from jax.sharding import PartitionSpec as P


def on_device(
    features,
    bases,
    root,
    coeffs,
    tiles,
    tile_dst,
    tile_src,
    tile_rel,
    tile_live,
    send_list,
    cotangent,
):
    highest = lax.Precision.HIGHEST
    contract_first = (((0,), (0,)), ((), ()))
    feat_width = features.shape[1]
    size_block = tiles.shape[-1]
    blocks = features.reshape(-1, size_block, feat_width)
    local_blocks = blocks.shape[0]
    num_bases = bases.shape[0]
    slots_peer = send_list.shape[-1]
    row_devices = lax.axis_size("rows")
    total_slots = row_devices * slots_peer
    count_tiles = tiles.shape[2]
    adjacency = tiles[0, 0]
    dst_ids = tile_dst[0, 0]
    src_ids = tile_src[0, 0]
    rel_ids = tile_rel[0, 0]
    live_count = tile_live[0, 0]
    send_rows = send_list[0, 0]
    outgoing = blocks[send_rows]
    incoming = lax.all_to_all(outgoing, "rows", split_axis=0, concat_axis=0, tiled=True)
    received = incoming.reshape(total_slots, size_block, feat_width)
    step_tiles = math.gcd(count_tiles, 64)
    steps_live = (live_count + step_tiles - 1) // step_tiles

    def tile_weights(first_tile):
        position = first_tile + jnp.arange(step_tiles)
        in_use = (position < live_count).astype(jnp.float32)
        rel_hot = (rel_ids[:, None] == jnp.arange(coeffs.shape[0])[None, :]).astype(jnp.float32)
        coef_rows = jnp.dot(rel_hot, coeffs, precision=highest)
        dst_hot = (dst_ids[:, None] == jnp.arange(local_blocks)[None, :]).astype(
            jnp.float32
        ) * in_use[:, None]
        return (dst_hot[:, :, None] * coef_rows[:, None, :]).reshape(
            step_tiles, local_blocks * num_bases
        )

    def forward_step(block_index, running):
        first_tile = block_index * step_tiles
        sources = received[src_ids]
        messages = jnp.einsum(
            "tij,tjf->tif", adjacency, sources, preferred_element_type=jnp.float32
        )
        weights = tile_weights(first_tile)
        return running + lax.dot_general(
            weights, messages.reshape(step_tiles, -1), contract_first, precision=highest
        )

    zero_total = jnp.zeros((local_blocks * num_bases, size_block * feat_width), jnp.float32)
    partial_value = lax.fori_loop(0, steps_live, forward_step, zero_total)
    partial_value = partial_value.reshape(local_blocks, num_bases, size_block, feat_width)
    basis_f32 = bases.astype(jnp.float32)
    cot_blocks = cotangent.reshape(local_blocks, size_block, feat_width)
    cot_f32 = cot_blocks.astype(jnp.float32)
    root_term = jnp.dot(features, root, preferred_element_type=jnp.float32)
    root_local = lax.dot_general(
        features, cotangent, contract_first, preferred_element_type=jnp.float32
    )
    aggregate = lax.psum(partial_value, "rel")
    projected = jnp.einsum("lbnf,bfg->lng", aggregate, basis_f32, precision=highest)
    basis_local = jnp.einsum("lbnf,lng->bfg", aggregate, cot_f32, precision=highest)
    basis_grad, root_grad = lax.psum((basis_local, root_local), "rows")
    output = (projected.reshape(-1, feat_width) + root_term).astype(jnp.bfloat16)
    agg_grad = jnp.einsum("lng,bfg->lbnf", cot_blocks, bases, preferred_element_type=jnp.float32)
    agg_grad = agg_grad.reshape(local_blocks * num_bases, size_block * feat_width)

    def backward_step(block_index, running):
        first_tile = block_index * step_tiles
        weights = tile_weights(first_tile)
        spread = jnp.dot(weights, agg_grad, precision=highest).astype(jnp.bfloat16)
        spread = spread.reshape(step_tiles, size_block, feat_width)
        backward_term = jnp.einsum(
            "tij,tif->tjf", adjacency, spread, preferred_element_type=jnp.float32
        )
        slot_hot = (src_ids[:, None] == jnp.arange(total_slots)[None, :]).astype(jnp.float32)
        return running + lax.dot_general(
            slot_hot, backward_term.reshape(step_tiles, -1), contract_first, precision=highest
        )

    slot_zero = jnp.zeros((total_slots, size_block * feat_width), jnp.float32)
    slot_grads = lax.fori_loop(0, steps_live, backward_step, slot_zero)
    returned = lax.all_to_all(
        slot_grads.reshape(row_devices, slots_peer, size_block * feat_width),
        "rows",
        split_axis=0,
        concat_axis=0,
        tiled=True,
    )
    block_hot = (send_rows.reshape(-1)[None, :] == jnp.arange(local_blocks)[:, None]).astype(
        jnp.float32
    )
    own_grads = jnp.dot(block_hot, returned.reshape(total_slots, -1), precision=highest)
    summed = lax.psum(own_grads, "rel")
    root_back = lax.dot_general(
        cotangent, root, (((1,), (1,)), ((), ())), preferred_element_type=jnp.float32
    )
    feature_grad = summed.reshape(-1, feat_width) + root_back
    return (output, feature_grad, basis_grad, root_grad)


def solution(mesh):
    return jax.shard_map(
        on_device,
        mesh=mesh,
        in_specs=(
            P("rows", None),
            P(),
            P(),
            P("rel", None),
            P("rows", "rel", None, None, None),
            P("rows", "rel", None),
            P("rows", "rel", None),
            P("rows", "rel", None),
            P("rows", "rel"),
            P("rows", "rel", None, None),
            P("rows", None),
        ),
        out_specs=(P("rows", None), P("rows", None), P(), P()),
        check_vma=False,
    )
```

profile of v0, /device:TPU:1, one launch (start us, length us, event | category | flops | bytes accessed | tf_op | source)
XLA Modules:
  0.0 457.6 jit_solution(15787599625584917114)
XLA Ops:
  8.2 3.7 gather_fusion
  11.9 9.6 %all-to-all-start = ((bf16[32,2,128,256]{3,2,1,0:T(8,128)(2,1)}), bf16[32,2,128,256]{3,2,1,0:T(8,128)(2,1)}, u32[]{:S(2)}, u32[]{:S(2)}) async-start(bf16[32,2,128,256]{3,2,1,0:T(8,128)(2,1)} %bitcast.130), calls=%async_computation | async-start | bytes 8388608 | tf_op jit(solution)/shard_map/all_to_all | solution.py:39
  22.2 2.7 convolution_bitcast_fusion.1
  24.9 5.5 %copy.36 = f32[4,8,128,256]{3,1,2,0:T(8,128)} copy(f32[4,8,128,256]{2,3,0,1:T(8,128)} %convolution_bitcast_fusion.1) | data formatting | bytes 8388608
  30.6 3.9 broadcast_in_dim.5
  34.5 38.4 %while.25 = (s32[]{:T(128)}, f32[64,32768]{1,0:T(8,128)}, s32[]{:T(128)}, s32[1,1,64]{2,1,0:T(1,128)S(1)}, s32[1,1,64]{2,1,0:T(1,128)S(1)}, /*index=5*/s32[]{:T(...) while((s32[]{:T(128)}, f32[64,32768]{1,0:T(8,128)}, ...), condition=%wide.region_4.5_spmd, body=%wide.region_3.4_spmd.sunk | while | flops 2956991232 | bytes 73405568 | solution.py:99
  35.4 8.6 %convolution_convert_fusion.2 = bf16[64,32768]{1,0:T(8,128)(2,1)S(1)} fusion(f32[32,32768]{1,0:T(8,128)} %get-tuple-element.440, f32[64,8]{0,1:T(8,128)S(1)} %get-tuple-element.439, f32[64,4]{0,1:T(4,128)S(1)} %fusion.64), kind=kOutput, calls=%fused_computation.11.clone.1 | convolution fusion | flops 807405568 | bytes 8391680 | tf_op jit(solution)/shard_map/while/body/dot_general | solution.py:88
  44.0 1.1 copy.45
  45.1 4.5 convolution_bitcast_fusion.4
  49.6 9.2 %copy.46 = f32[8,8,128,256]{3,1,2,0:T(8,128)} copy(f32[8,8,128,256]{2,3,1,0:T(8,128)} %bitcast.122) | data formatting | bytes 16777216 | tf_op jit(solution)/shard_map/while
  58.8 14.1 %convolution_add_fusion.7 = f32[64,32768]{1,0:T(8,128)} fusion(f32[64,32768]{1,0:T(8,128)} %get-tuple-element.423, f32[64,32768]{1,0:T(8,128)} %bitcast.121, s32[64]{0:T(128)S(1)} %bitcast.136), kind=kOutput, calls=%fused_computation.10.clone.1 | convolution fusion | flops 1612713984 | bytes 25166080 | tf_op jit(solution)/shard_map/while/body/dot_general | solution.py:94
  72.9 10.6 %reshape.243 = f32[32,2,32768]{2,1,0:T(2,128)} reshape(f32[64,32768]{1,0:T(8,128)} %get-tuple-element.236) | data formatting | bytes 16777216 | tf_op jit(solution)/shard_map/reshape | solution.py:101
  83.6 7.6 %all-to-all-start.1 = ((f32[32,2,32768]{2,1,0:T(2,128)}), f32[32,2,32768]{2,1,0:T(2,128)}, u32[]{:S(2)}, u32[]{:S(2)}) async-start(f32[32,2,32768]{2,1,0:T(2,128)} %reshape.243), calls=%async_computation.1 | async-start | bytes 16777216 | tf_op jit(solution)/shard_map/all_to_all | solution.py:100
  91.4 4.9 %gather_fusion.1 = bf16[64,128,256]{2,1,0:T(8,128)(2,1)} fusion(bf16[64,128,256]{2,1,0:T(8,128)(2,1)} %bitcast.12, s32[1024]{0:T(1024)S(1)} %pad_clamp_fusion), kind=kCustom, calls=%fused_computation.1 | custom fusion | bytes 8388864 | tf_op jit(solution)/shard_map/while/body/gather | solution.py:58
  96.3 2.3 broadcast_in_dim.4
  98.6 16.0 %while.24 = (s32[]{:T(128)}, f32[32,32768]{1,0:T(8,128)}, s32[]{:T(128)}, s32[1,1,64]{2,1,0:T(1,128)S(1)}, s32[]{:T(128)}, /*index=5*/f32[64,8]{0,1:T(8,128)S(1)...) while((s32[]{:T(128)}, f32[32,32768]{1,0:T(8,128)}, s32[]{:T(128)}, ...), condition=%wide.region_1.2_spmd, body=%wide.region_0.1_spmd.sunk | while | flops 1343228672 | bytes 48239480 | solution.py:68
  99.3 3.4 fusion.57
  102.7 4.7 %copy.44 = f32[8,8,128,256]{3,1,2,0:T(8,128)S(1)} copy(f32[8,8,128,256]{3,2,1,0:T(8,128)S(1)} %bitcast.123) | data formatting | bytes 16777216 | tf_op jit(solution)/shard_map/while
  107.5 7.1 %convolution_add_fusion.6 = f32[32,32768]{1,0:T(8,128)} fusion(f32[32,32768]{1,0:T(8,128)} %get-tuple-element.392, f32[64,32768]{1,0:T(8,128)S(1)} %bitcast.120, f32[64,8]{0,1:T(8,128)S(1)} %get-tuple-element.406, f32[64,4]{0,1:T(4,128)S(1)} %fusion.58), kind=kOutput, calls=%fused_computation.2.clone.1 | convolution fusion | flops 806356992 | bytes 16780288 | tf_op jit(solution)/shard_map/while/body/dot_general | solution.py:63
  114.6 5.4 %copy.40 = f32[4,8,128,256]{3,2,1,0:T(8,128)} copy(f32[4,8,128,256]{3,1,2,0:T(8,128)} %bitcast.127) | data formatting | bytes 8388608
  120.0 78.3 %all-to-all-done.1 = f32[32,2,32768]{2,1,0:T(2,128)} async-done(((f32[32,2,32768]{2,1,0:T(2,128)}), f32[32,2,32768]{2,1,0:T(2,128)}, u32[]{:S(2)}, u32[]{:S(2)}) %all-to-all-start.1) | async-done | bytes 8388640 | tf_op jit(solution)/shard_map/all_to_all | solution.py:100
  198.3 10.9 %reshape.244 = f32[64,32768]{1,0:T(8,128)} reshape(f32[32,2,32768]{2,1,0:T(2,128)} %all-to-all-done.1) | data formatting | bytes 16777216 | tf_op jit(solution)/shard_map/reshape | solution.py:110
  209.3 6.2 %fusion.17 = f32[4,32768]{1,0:T(4,128)S(1)} fusion(f32[64,32768]{1,0:T(8,128)} %reshape.244, s32[64]{0:T(128)S(1)} %eq.116), kind=kOutput, calls=%fused_computation.39 | convolution fusion | flops 100663552 | bytes 8913152 | tf_op jit(solution)/shard_map/dot_general | solution.py:110
  215.5 1.2 reshape.245
  216.7 1.0 fusion.21
  217.7 114.5 %all-reduce.7.cloned.1.call-done = (f32[4,8,128,256]{3,2,1,0:T(8,128)}, f32[512,256]{1,0:T(8,128)}) async-done(((f32[4,8,128,256]{3,2,1,0:T(8,128)}, f32[512,256]{1,0:T(8,128)}), (f32[4,8,128,256]{3,2,1,0:T(8,128)}, f32[512,256]{1,0:T(8,128)})) %all-reduce.7.cloned.1.call-update) | async-done | bytes 4718608 | tf_op jit(solution)/shard_map/psum | solution.py:77
  332.1 6.9 %convolution_bitcast_fusion.2 = f32[8,256,256]{2,1,0:T(8,128)} fusion(f32[4,8,128,256]{3,2,1,0:T(8,128)} %get-tuple-element.273, bf16[4,128,256,1]{2,1,3,0:T(8,128)(2,1)S(1)} %bitcast.132), kind=kOutput, calls=%fused_computation.24 | convolution fusion | flops 3221225472 | bytes 6553600 | tf_op jit(solution)/shard_map/lbnf,lng->bfg/dot_general | solution.py:79
  339.1 4.3 fusion.13
  343.4 0.9 fusion.11
  344.3 1.1 convolution_add_fusion.2
  345.4 101.6 %all-reduce.5.cloned.1.call-done = (f32[8,256,256]{2,1,0:T(8,128)}, f32[256,256]{1,0:T(8,128)}) async-done(((f32[8,256,256]{2,1,0:T(8,128)}, f32[256,256]{1,0:T(8,128)}), (f32[8,256,256]{2,1,0:T(8,128)}, f32[256,256]{1,0:T(8,128)})) %all-reduce.5.cloned.1.call-update) | async-done | bytes 2359312 | tf_op jit(solution)/shard_map/psum | solution.py:80
  447.0 3.1 copy.65
  (45 shorter events, 3.6 us)
Async XLA Ops:
  7.2 15.0 %copy-start = (bf16[8,256,256]{2,1,0:T(8,128)(2,1)S(1)}, bf16[8,256,256]{2,1,0:T(8,128)(2,1)}, u32[]{:S(2)}) copy-start(bf16[8,256,256]{2,1,0:T(8,128)(2,1)} %param.16) | copy-start | bytes 3145732
  11.9 10.3 %copy-start.3 = (bf16[512,256]{1,0:T(8,128)(2,1)S(1)}, bf16[512,256]{1,0:T(8,128)(2,1)}, u32[]{:S(2)}) copy-start(bf16[512,256]{1,0:T(8,128)(2,1)} %param.25) | copy-start | bytes 786436
  11.9 71.7 %all-to-all-start = ((bf16[32,2,128,256]{3,2,1,0:T(8,128)(2,1)}), bf16[32,2,128,256]{3,2,1,0:T(8,128)(2,1)}, u32[]{:S(2)}, u32[]{:S(2)}) async-start(bf16[32,2,128,256]{3,2,1,0:T(8,128)(2,1)} %bitcast.130), calls=%async_computation | async-start | bytes 8388608 | tf_op jit(solution)/shard_map/all_to_all | solution.py:39
  24.9 5.5 %copy-start.11 = (f32[200,8]{0,1:T(8,128)S(1)}, f32[200,8]{0,1:T(8,128)}, u32[]{:S(2)}) copy-start(f32[200,8]{0,1:T(8,128)} %param.18) | copy-start | bytes 19204
  24.9 5.5 %copy-start.12 = (s32[1,1,64]{2,1,0:T(1,128)S(1)}, s32[1,1,64]{2,1,0:T(1,128)}, u32[]{:S(2)}) copy-start(s32[1,1,64]{2,1,0:T(1,128)} %param.22) | copy-start | bytes 772
  30.6 4.0 copy-start.1
  30.6 4.0 copy-start.8
  30.6 4.0 copy-start.9
  83.6 7.6 %copy-start.10 = (s32[1,1,32,2]{2,3,1,0:T(2,128)S(1)}, s32[1,1,32,2]{2,3,1,0:T(2,128)}, u32[]{:S(2)}) copy-start(s32[1,1,32,2]{2,3,1,0:T(2,128)} %param.24) | copy-start | bytes 772
  83.6 114.8 %all-to-all-start.1 = ((f32[32,2,32768]{2,1,0:T(2,128)}), f32[32,2,32768]{2,1,0:T(2,128)}, u32[]{:S(2)}, u32[]{:S(2)}) async-start(f32[32,2,32768]{2,1,0:T(2,128)} %reshape.243), calls=%async_computation.1 | async-start | bytes 16777216 | tf_op jit(solution)/shard_map/all_to_all | solution.py:100
  91.1 241.0 %all-reduce.7.cloned.1.call-start = ((), (), s32[]{:S(2)}) async-start(), calls=%async_computation.3 | async-start | bytes 9437184 | tf_op jit(solution)/shard_map/psum | solution.py:77
  215.4 1.2 copy-start.2
  215.5 1.3 copy-start.4
  216.6 230.3 %all-reduce.5.cloned.1.call-start = ((), (), s32[]{:S(2)}) async-start(), calls=%async_computation.2 | async-start | bytes 4718592 | tf_op jit(solution)/shard_map/psum | solution.py:80
  339.1 4.3 copy-start.6
  339.1 5.2 %copy-start.5 = (f32[512,256]{1,0:T(8,128)S(1)}, f32[512,256]{1,0:T(8,128)}, u32[]{:S(2)}) copy-start(f32[512,256]{1,0:T(8,128)} %get-tuple-element.274) | copy-start | bytes 1572868
  447.0 3.1 copy-start.7
Sparse Core Ops, SparseCore 0:
  216.8 115.3 all-reduce.6
  339.2 107.6 all-reduce.4
where the time goes:
time: 459 us; the launch traced here: 458 us
  waiting for transfers between devices  294 us (64%)
  local copies, waits for them, and re-layouts  67.8 us (15%)
  matrix products  60.9 us (13%)
  starting transfers between devices  17.3 us (4%)
  between operations  14.8 us (3%)
    psum x1, waiting for transfers between devices, on_device(): aggregate = lax.psum(partial_value, 'rel')  114 us
    psum x1, waiting for transfers between devices, on_device(): basis_grad, root_grad = lax.psum((basis_local, root_local), 'rows')  102 us
    all_to_all x1, waiting for transfers between devices, on_device(): lax.all_to_all(slot_grads.reshape(row_devices, slots_peer, size_block * f...  78.3 us
    while x3, local copies, waits for them, and re-layouts  15 us
    unnamed x31, local copies, waits for them, and re-layouts  14.9 us
    dot_general x1, matrix products, backward_step(): lax.dot_general(slot_hot, backward_term.reshape(step_tiles, -1), contract...  14.1 us
    reshape x1, local copies, waits for them, and re-layouts, on_device(): returned.reshape(total_slots, -1)  10.9 us
    reshape x1, local copies, waits for them, and re-layouts, on_device(): slot_grads.reshape(row_devices, slots_peer, size_block * feat_width)  10.6 us
  transfers between devices with their start and end apart: 4, of which 3 were waited for; matrix products, arithmetic and copies ran while one was open for 21% of the time, Pallas kernels for 0%

commit v1 on v0

--- a/solution.py
+++ b/solution.py
@@ -74,7 +74,7 @@
     root_local = lax.dot_general(
         features, cotangent, contract_first, preferred_element_type=jnp.float32
     )
-    aggregate = lax.psum(partial_value, "rel")
+    aggregate = jnp.sum(lax.all_gather(partial_value, axis_name="rel"), axis=0)
     projected = jnp.einsum("lbnf,bfg->lng", aggregate, basis_f32, precision=highest)
     basis_local = jnp.einsum("lbnf,lng->bfg", aggregate, cot_f32, precision=highest)
     basis_grad, root_grad = lax.psum((basis_local, root_local), "rows")

time: 459 us -> 488 us (1.063); the launches traced: 458 us -> 479 us
  other arithmetic: 2.1 us -> 12 us
  local copies, waits for them, and re-layouts: 67.8 us -> 74.5 us
  waiting for transfers between devices: 294 us -> 299 us
    psum x1, waiting for transfers between devices: 114 us -> 37.4 us  [on_device(): summed = lax.psum(own_grads, 'rel')]
    all_to_all x1, waiting for transfers between devices: 0.01 us -> 51.2 us  [on_device(): lax.all_to_all(outgoing, 'rows', split_axis=0, concat_axis=0, tiled=True)]
    all_to_all x1, waiting for transfers between devices: 78.3 us -> 107 us  [on_device(): lax.all_to_all(slot_grads.reshape(row_devices, slots_peer, size_block * f...]
    reduce_sum x0 -> x1, other arithmetic: none -> 9.85 us  [on_device(): aggregate = jnp.sum(lax.all_gather(partial_value, axis_name='rel'), axis=0)]
    unnamed x31 -> x27, local copies, waits for them, and re-layouts: 14.9 us -> 15.9 us
  transfers between devices with their start and end apart: 4 -> 5, of which waited for: 3 -> 4; matrix products, arithmetic and copies ran while one was open for 21% -> 23% of each run, Pallas kernels for 0% -> 0%
where the time goes in v1:
time: 488 us; the launch traced here: 479 us
  waiting for transfers between devices  299 us (61%)
  local copies, waits for them, and re-layouts  74.5 us (15%)
  matrix products  61.2 us (13%)
  starting transfers between devices  16.9 us (3%)
  between operations  14.9 us (3%)
  other arithmetic  12 us (2%)
    all_to_all x1, waiting for transfers between devices, on_device(): lax.all_to_all(slot_grads.reshape(row_devices, slots_peer, size_block * f...  107 us
    psum x1, waiting for transfers between devices, on_device(): basis_grad, root_grad = lax.psum((basis_local, root_local), 'rows')  104 us
    all_to_all x1, waiting for transfers between devices, on_device(): lax.all_to_all(outgoing, 'rows', split_axis=0, concat_axis=0, tiled=True)  51.2 us
    psum x1, waiting for transfers between devices, on_device(): summed = lax.psum(own_grads, 'rel')  37.4 us
    unnamed x27, local copies, waits for them, and re-layouts  15.9 us
    while x3, local copies, waits for them, and re-layouts  15.1 us
    dot_general x1, matrix products, backward_step(): lax.dot_general(slot_hot, backward_term.reshape(step_tiles, -1), contract...  14.1 us
    reshape x1, local copies, waits for them, and re-layouts, on_device(): returned.reshape(total_slots, -1)  10.9 us
  transfers between devices with their start and end apart: 5, of which 4 were waited for; matrix products, arithmetic and copies ran while one was open for 23% of the time, Pallas kernels for 0%

profile of v1, /device:TPU:1, one launch (start us, length us, event | category | flops | bytes accessed | tf_op | source)
XLA Modules:
  0.0 479.1 jit_solution(5645427993196151722)
XLA Ops:
  8.2 3.7 gather_fusion
  11.9 9.6 %all-to-all-start = ((bf16[32,2,128,256]{3,2,1,0:T(8,128)(2,1)}), bf16[32,2,128,256]{3,2,1,0:T(8,128)(2,1)}, u32[]{:S(2)}, u32[]{:S(2)}) async-start(bf16[32,2,128,256]{3,2,1,0:T(8,128)(2,1)} %bitcast.130), calls=%async_computation | async-start | bytes 8388608 | tf_op jit(solution)/shard_map/all_to_all | solution.py:39
  22.5 51.2 %all-to-all-done = bf16[32,2,128,256]{3,2,1,0:T(8,128)(2,1)} async-done(((bf16[32,2,128,256]{3,2,1,0:T(8,128)(2,1)}), bf16[32,2,128,256]{3,2,1,0:T(8,128)(2,1)}, u32[]{:S(2)}, u32[]{:S(2)}) %all-to-all-start) | async-done | bytes 4194336 | tf_op jit(solution)/shard_map/all_to_all | solution.py:39
  73.6 5.0 %gather_fusion.1 = bf16[64,128,256]{2,1,0:T(8,128)(2,1)} fusion(bf16[64,128,256]{2,1,0:T(8,128)(2,1)} %bitcast.12, s32[1024]{0:T(1024)S(1)} %pad_clamp_fusion), kind=kCustom, calls=%fused_computation.1 | custom fusion | bytes 8388864 | tf_op jit(solution)/shard_map/while/body/gather | solution.py:58
  78.6 2.3 broadcast_in_dim.4
  81.0 16.1 %while.24 = (s32[]{:T(128)}, f32[32,32768]{1,0:T(8,128)}, s32[]{:T(128)}, s32[1,1,64]{2,1,0:T(1,128)S(1)}, s32[]{:T(128)}, /*index=5*/f32[64,8]{0,1:T(8,128)S(1)...) while((s32[]{:T(128)}, f32[32,32768]{1,0:T(8,128)}, s32[]{:T(128)}, ...), condition=%wide.region_1.2_spmd, body=%wide.region_0.1_spmd.sunk | while | flops 1343228672 | bytes 48239480 | solution.py:68
  81.7 3.4 fusion.60
  85.1 4.7 copy.62
  89.9 7.1 %convolution_add_fusion.6 = f32[32,32768]{1,0:T(8,128)} fusion(f32[32,32768]{1,0:T(8,128)} %get-tuple-element.390, f32[64,32768]{1,0:T(8,128)S(1)} %bitcast.118, f32[64,8]{0,1:T(8,128)S(1)} %get-tuple-element.404, f32[64,4]{0,1:T(4,128)S(1)} %fusion.61), kind=kOutput, calls=%fused_computation.2.clone.1 | convolution fusion | flops 806356992 | bytes 16780288 | tf_op jit(solution)/shard_map/while/body/dot_general | solution.py:63
  97.2 5.4 %copy.58 = f32[4,8,128,256]{3,2,1,0:T(8,128)} copy(f32[4,8,128,256]{3,1,2,0:T(8,128)} %bitcast.125) | data formatting | bytes 8388608
  103.5 2.7 convolution_bitcast_fusion.1
  106.2 5.5 %copy.50 = f32[4,8,128,256]{3,1,2,0:T(8,128)} copy(f32[4,8,128,256]{2,3,0,1:T(8,128)} %convolution_bitcast_fusion.1) | data formatting | bytes 8388608
  111.7 5.0 %broadcast_in_dim.5 = f32[64,32768]{1,0:T(8,128)} broadcast(f32[]{:T(128)} %constant.52.clone.1), dimensions={} | broadcast | bytes 8388612 | tf_op jit(solution)/shard_map/broadcast_in_dim | solution.py:98
  116.7 38.5 %while.25 = (s32[]{:T(128)}, f32[64,32768]{1,0:T(8,128)}, s32[]{:T(128)}, s32[1,1,64]{2,1,0:T(1,128)S(1)}, s32[1,1,64]{2,1,0:T(1,128)S(1)}, /*index=5*/s32[]{:T(...) while((s32[]{:T(128)}, f32[64,32768]{1,0:T(8,128)}, ...), condition=%wide.region_4.5_spmd, body=%wide.region_3.4_spmd.sunk | while | flops 2956991232 | bytes 73405568 | solution.py:99
  117.3 8.8 %convolution_convert_fusion.2 = bf16[64,32768]{1,0:T(8,128)(2,1)S(1)} fusion(f32[32,32768]{1,0:T(8,128)} %get-tuple-element.438, f32[64,8]{0,1:T(8,128)S(1)} %get-tuple-element.437, f32[64,4]{0,1:T(4,128)S(1)} %fusion.67), kind=kOutput, calls=%fused_computation.11.clone.1 | convolution fusion | flops 807405568 | bytes 8391680 | tf_op jit(solution)/shard_map/while/body/dot_general | solution.py:88
  127.3 4.6 convolution_bitcast_fusion.4
  131.8 9.2 %copy.64 = f32[8,8,128,256]{3,1,2,0:T(8,128)} copy(f32[8,8,128,256]{2,3,1,0:T(8,128)} %bitcast.120) | data formatting | bytes 16777216 | tf_op jit(solution)/shard_map/while
  141.1 14.1 %convolution_add_fusion.7 = f32[64,32768]{1,0:T(8,128)} fusion(f32[64,32768]{1,0:T(8,128)} %get-tuple-element.421, f32[64,32768]{1,0:T(8,128)} %bitcast.119, s32[64]{0:T(128)S(1)} %bitcast.136), kind=kOutput, calls=%fused_computation.10.clone.1 | convolution fusion | flops 1612713984 | bytes 25166080 | tf_op jit(solution)/shard_map/while/body/dot_general | solution.py:94
  155.2 10.7 %reshape.237 = f32[32,2,32768]{2,1,0:T(2,128)} reshape(f32[64,32768]{1,0:T(8,128)} %get-tuple-element.236) | data formatting | bytes 16777216 | tf_op jit(solution)/shard_map/reshape | solution.py:101
  165.9 7.2 %all-to-all-start.1 = ((f32[32,2,32768]{2,1,0:T(2,128)}), f32[32,2,32768]{2,1,0:T(2,128)}, u32[]{:S(2)}, u32[]{:S(2)}) async-start(f32[32,2,32768]{2,1,0:T(2,128)} %reshape.237), calls=%async_computation.1 | async-start | bytes 16777216 | tf_op jit(solution)/shard_map/all_to_all | solution.py:100
  173.3 106.9 %all-to-all-done.1 = f32[32,2,32768]{2,1,0:T(2,128)} async-done(((f32[32,2,32768]{2,1,0:T(2,128)}), f32[32,2,32768]{2,1,0:T(2,128)}, u32[]{:S(2)}, u32[]{:S(2)}) %all-to-all-start.1) | async-done | bytes 8388640 | tf_op jit(solution)/shard_map/all_to_all | solution.py:100
  280.3 10.9 %reshape.238 = f32[64,32768]{1,0:T(8,128)} reshape(f32[32,2,32768]{2,1,0:T(2,128)} %all-to-all-done.1) | data formatting | bytes 16777216 | tf_op jit(solution)/shard_map/reshape | solution.py:110
  291.2 6.2 %fusion.20 = f32[4,32768]{1,0:T(4,128)S(1)} fusion(f32[64,32768]{1,0:T(8,128)} %reshape.238, s32[64]{0:T(128)S(1)} %eq.116), kind=kOutput, calls=%fused_computation.40 | convolution fusion | flops 100663552 | bytes 8913152 | tf_op jit(solution)/shard_map/dot_general | solution.py:110
  297.4 1.2 reshape.239
  299.6 9.8 %reduce_sum.9 = f32[4,8,128,256]{3,2,1,0:T(8,128)} reduce(f32[4,4,8,128,256]{4,3,2,1,0:T(8,128)} %all-gather.2.cloned.1.call-done, f32[]{:T(128)} %constant.52.clone.1), dimensions={0}, to_apply=%region_2.3 | reduce | flops 3145728 | bytes 20971524 | tf_op jit(solution)/shard_map/reduce_sum | solution.py:77
  309.4 7.0 %convolution_bitcast_fusion.2 = f32[8,256,256]{2,1,0:T(8,128)} fusion(f32[4,8,128,256]{3,2,1,0:T(8,128)} %reduce_sum.9, bf16[4,128,256,1]{2,1,3,0:T(8,128)(2,1)S(1)} %bitcast.133), kind=kOutput, calls=%fused_computation.26 | convolution fusion | flops 3221225472 | bytes 6553600 | tf_op jit(solution)/shard_map/lbnf,lng->bfg/dot_general | solution.py:79
  316.4 37.4 %all-reduce.4.cloned.1.call-done = f32[512,256]{1,0:T(8,128)} async-done(((f32[512,256]{1,0:T(8,128)}), f32[512,256]{1,0:T(8,128)}) %all-reduce.4.cloned.1.call-update) | async-done | bytes 524304 | tf_op jit(solution)/shard_map/psum | solution.py:111
  353.8 2.1 convolution_add_fusion.2
  355.9 4.6 copy.37
  360.6 3.0 fusion.13
  364.5 103.8 %all-reduce.6.cloned.1.call-done = (f32[8,256,256]{2,1,0:T(8,128)}, f32[256,256]{1,0:T(8,128)}) async-done(((f32[8,256,256]{2,1,0:T(8,128)}, f32[256,256]{1,0:T(8,128)}), (f32[8,256,256]{2,1,0:T(8,128)}, f32[256,256]{1,0:T(8,128)})) %all-reduce.6.cloned.1.call-update) | async-done | bytes 2359312 | tf_op jit(solution)/shard_map/psum | solution.py:80
  468.4 3.1 copy.82
  (46 shorter events, 7.7 us)
Async XLA Ops:
  7.2 95.4 %copy-start = (bf16[8,256,256]{2,1,0:T(8,128)(2,1)S(1)}, bf16[8,256,256]{2,1,0:T(8,128)(2,1)}, u32[]{:S(2)}) copy-start(bf16[8,256,256]{2,1,0:T(8,128)(2,1)} %param.16) | copy-start | bytes 3145732
  11.9 10.3 %copy-start.7 = (s32[1,1,64]{2,1,0:T(1,128)S(1)}, s32[1,1,64]{2,1,0:T(1,128)}, u32[]{:S(2)}) copy-start(s32[1,1,64]{2,1,0:T(1,128)} %param.21) | copy-start | bytes 772
  11.9 10.4 %copy-start.9 = (f32[200,8]{0,1:T(8,128)S(1)}, f32[200,8]{0,1:T(8,128)}, u32[]{:S(2)}) copy-start(f32[200,8]{0,1:T(8,128)} %param.18) | copy-start | bytes 19204
  11.9 10.4 %copy-start.10 = (s32[1,1,64]{2,1,0:T(1,128)S(1)}, s32[1,1,64]{2,1,0:T(1,128)}, u32[]{:S(2)}) copy-start(s32[1,1,64]{2,1,0:T(1,128)} %param.22) | copy-start | bytes 772
  11.9 61.7 %all-to-all-start = ((bf16[32,2,128,256]{3,2,1,0:T(8,128)(2,1)}), bf16[32,2,128,256]{3,2,1,0:T(8,128)(2,1)}, u32[]{:S(2)}, u32[]{:S(2)}) async-start(bf16[32,2,128,256]{3,2,1,0:T(8,128)(2,1)} %bitcast.130), calls=%async_computation | async-start | bytes 8388608 | tf_op jit(solution)/shard_map/all_to_all | solution.py:39
  21.5 278.1 %all-gather.2.cloned.1.call-start = ((), (), s32[]{:S(2)}) async-start(), calls=%async_computation.2 | async-start | bytes 20971520 | tf_op jit(solution)/shard_map/all_gather | solution.py:77
  78.6 2.4 copy-start.1
  78.6 2.4 copy-start.6
  102.6 0.9 copy-start.3
  165.9 7.3 %copy-start.8 = (s32[1,1,32,2]{2,3,1,0:T(2,128)S(1)}, s32[1,1,32,2]{2,3,1,0:T(2,128)}, u32[]{:S(2)}) copy-start(s32[1,1,32,2]{2,3,1,0:T(2,128)} %param.24) | copy-start | bytes 772
  165.9 114.4 %all-to-all-start.1 = ((f32[32,2,32768]{2,1,0:T(2,128)}), f32[32,2,32768]{2,1,0:T(2,128)}, u32[]{:S(2)}, u32[]{:S(2)}) async-start(f32[32,2,32768]{2,1,0:T(2,128)} %reshape.237), calls=%async_computation.1 | async-start | bytes 16777216 | tf_op jit(solution)/shard_map/all_to_all | solution.py:100
  173.1 180.8 %all-reduce.4.cloned.1.call-start = ((), (), s32[]{:S(2)}) async-start(), calls=%async_computation.3 | async-start | bytes 1048576 | tf_op jit(solution)/shard_map/psum | solution.py:111
  291.2 7.4 %copy-start.2 = (bf16[512,256]{1,0:T(8,128)(2,1)S(1)}, bf16[512,256]{1,0:T(8,128)(2,1)}, u32[]{:S(2)}) copy-start(bf16[512,256]{1,0:T(8,128)(2,1)} %param.15) | copy-start | bytes 786436
  298.6 169.8 %all-reduce.6.cloned.1.call-start = ((), (), s32[]{:S(2)}) async-start(), calls=%async_computation.4 | async-start | bytes 4718592 | tf_op jit(solution)/shard_map/psum | solution.py:80
  309.4 44.4 %copy-start.4 = (bf16[256,256]{1,0:T(8,128)(2,1)S(1)}, bf16[256,256]{1,0:T(8,128)(2,1)}, u32[]{:S(2)}) copy-start(bf16[256,256]{1,0:T(8,128)(2,1)} %param.17) | copy-start | bytes 393220
  468.3 3.1 copy-start.5
Sparse Core Ops, SparseCore 0:
  102.7 154.6 all-gather.1
  298.7 55.1 all-reduce.3
  357.8 110.4 all-reduce.5
